TPU v7x, 32 devices: a whole 2x2x4 slice. The times are simulated.
32 devices in a mesh: section: 4 (over x, core), obs: 8 (over z, y).
Axes of the slice: x: 2, y: 2, z: 4, core: 2. Of those that a mesh axis runs over, the one named last changes fastest.
Arguments:
- predictors: bfloat16 [4, 4, 20, 32768], P('section', None, None, 'obs'), may hold values from -5 to 5
- departures: float32 [4, 4, 32768], P('section', None, 'obs'), may hold values from -30 to 30
- obs_precision: float32 [4, 4, 32768], P('section', None, 'obs'), may hold values from 0.3 to 3
- qc_pass: int32 [4, 4, 32768], P('section', None, 'obs'), may hold values 0 or 1
- block_channel: int32 [4, 4, 256], P('section', None, 'obs'), may hold values from 0 to 2047, as said below
- stream_order: int32 [4], replicated, may hold values from 0 to 3, each once
- prior_coeffs: float32 [4, 20, 2048], P(None, None, 'obs'), may hold values from -1 to 1
- prior_info: float32 [4, 210, 2048], P(None, None, 'obs'), may hold values from -1 to 32, as said below
- memory_factor: float32 [2048], P('obs'), may hold values from 0.5 to 0.98
Outputs:
- coeffs: float32 [4, 4, 20, 2048], P('section', None, None, 'obs')
- information: float32 [4, 4, 210, 2048], P('section', None, None, 'obs')
Inputs may be any that keep to these rules, and one draw needn't show every extreme that they name: `block_channel`: among the 32 row blocks of one index of obs, at most 8 have channels in any one range of the 256 channels from a multiple of 256; in every window and stream one such range holds exactly 8 blocks of every index of obs. `stream_order`: each stream appears once. `prior_info`: for every stream and channel the 210 entries are the upper triangle, row by row, of a symmetric positive definite matrix of order 20.
All inputs are finite; a program needn't handle non-finite values. No bound on the sum of `qc_pass` on one device may be relied on, other than what follows from the above.
Results may differ from a plain program's by a relative error of at most 0.0038.
Values sent between devices are 32-bit elements; how exact they have to be, the bound alone decides.
A program may use at most 64 MiB of HBM per device.

v0:
```python
import jax
import jax.numpy as jnp
import numpy as np
from jax import lax
from jax.sharding import PartitionSpec as P

HUBER_SQ = 9.0
PRIOR_WEIGHT = 64.0


def from_behind(array, axis, by):
    size = lax.axis_size(axis)
    pairs = [(i, i + by) for i in range(size) if 0 <= i + by < size]
    return lax.ppermute(array, axis, pairs)


def upper_positions(dimension):
    return np.array(
        [i * dimension + j for i in range(dimension) for j in range(i, dimension)], dtype=np.int32
    )


def solve_packed(packed, target):
    dimension = target.shape[0]
    placing = {}
    counter = 0
    for i in range(dimension):
        for j in range(i, dimension):
            placing[i, j] = counter
            counter += 1
    factor = [[None] * dimension for i in range(dimension)]
    for j in range(dimension):
        pivot_root = jnp.sqrt(
            packed[placing[j, j]] - sum((factor[j][k] * factor[j][k] for k in range(j)))
        )
        factor[j][j] = pivot_root
        for i in range(j + 1, dimension):
            factor[i][j] = (
                packed[placing[j, i]] - sum((factor[i][k] * factor[j][k] for k in range(j)))
            ) / pivot_root
    forward = []
    for i in range(dimension):
        forward.append(
            (target[i] - sum((factor[i][k] * forward[k] for k in range(i)))) / factor[i][i]
        )
    backward = [None] * dimension
    for i in reversed(range(dimension)):
        backward[i] = (
            forward[i] - sum((factor[k][i] * backward[k] for k in range(i + 1, dimension)))
        ) / factor[i][i]
    return jnp.stack(backward)


def block_terms(predicted, departed, precision, passed, block_coeffs):
    pred_count, row_count = predicted.shape
    block_count = block_coeffs.shape[1]
    block_width = row_count // block_count
    upper_index = upper_positions(pred_count)
    shaped = predicted.reshape(pred_count, block_count, block_width)
    offset = jnp.sum(shaped.astype(jnp.float32) * block_coeffs[:, :, None], axis=0)
    residual = departed.reshape(block_count, block_width) - offset
    scale_row = precision.reshape(block_count, block_width)
    weight = (
        passed.reshape(block_count, block_width).astype(jnp.float32)
        * scale_row
        / (1.0 + scale_row * residual * residual / HUBER_SQ)
    )
    weighted = (weight[None] * shaped.astype(jnp.float32)).astype(jnp.bfloat16)
    chi_square = jnp.sum(weight * residual * residual)
    passed_count = jnp.sum(passed.astype(jnp.float32))
    gram_full = lax.dot_general(
        weighted, shaped, (((2,), (2,)), ((1,), (1,))), preferred_element_type=jnp.float32
    )
    gram_upper = gram_full.reshape(block_count, pred_count * pred_count)[:, upper_index]
    gradient = jnp.sum(weighted.astype(jnp.float32) * residual[None], axis=2).T
    return (jnp.concatenate([gram_upper, gradient], axis=1), jnp.stack([chi_square, passed_count]))


def local(
    predictors,
    departures,
    obs_precision,
    qc_pass,
    block_channel,
    stream_order,
    prior_coeffs,
    prior_info,
    memory_factor,
):
    section_count = lax.axis_size("section")
    obs_devices = lax.axis_size("obs")
    section_place = lax.axis_index("section")
    stream_count = stream_order.shape[0]
    local_channels = memory_factor.shape[0]
    block_count = block_channel.shape[2]
    pred_count = prior_coeffs.shape[1]
    tri_count = prior_info.shape[1]
    column_count = tri_count + pred_count
    capacity = 2 * block_count // obs_devices
    local_line = jnp.arange(local_channels, dtype=jnp.float32)
    owner_line = jnp.arange(obs_devices, dtype=jnp.int32)
    slot_line = jnp.arange(obs_devices * capacity, dtype=jnp.int32)
    highest = lax.Precision.HIGHEST

    def pack_blocks(block_sums, channel):
        owner_index = channel // local_channels
        inner_channel = channel % local_channels
        owner_hot = (owner_index[:, None] == owner_line[None, :]).astype(jnp.int32)
        ranking = jnp.sum((jnp.cumsum(owner_hot, axis=0) - 1) * owner_hot, axis=1)
        slot_of = owner_index * capacity + ranking
        placing = (slot_of[:, None] == slot_line[None, :]).astype(jnp.float32)
        send_rows = lax.dot_general(
            placing,
            block_sums,
            (((0,), (0,)), ((), ())),
            precision=highest,
            preferred_element_type=jnp.float32,
        ).reshape(obs_devices, capacity, column_count)
        send_channel = (
            lax.dot_general(
                placing,
                (inner_channel + 1).astype(jnp.float32),
                (((0,), (0,)), ((), ())),
                precision=highest,
                preferred_element_type=jnp.float32,
            ).reshape(obs_devices, capacity)
            - 1.0
        )
        return (send_rows, send_channel)

    def unpack_blocks(got_rows, got_channel):
        gather_hot = (got_channel.reshape(-1)[:, None] == local_line[None, :]).astype(jnp.float32)
        return lax.dot_general(
            got_rows.reshape(-1, column_count),
            gather_hot,
            (((0,), (0,)), ((), ())),
            precision=highest,
            preferred_element_type=jnp.float32,
        )

    def window_work(state_now, streams):
        beta_prior = state_now[:, :pred_count]
        info_prior = state_now[:, pred_count:]
        all_coeffs = lax.all_gather(beta_prior, "obs", axis=2, tiled=True)
        channel = jnp.take(block_channel[0], streams, axis=0)
        block_coeffs = jax.vmap(lambda coeff_rows, chan: jnp.take(coeff_rows, chan, axis=1))(
            all_coeffs, channel
        )
        block_sums, statistics = jax.vmap(block_terms)(
            jnp.take(predictors[0], streams, axis=0),
            jnp.take(departures[0], streams, axis=0),
            jnp.take(obs_precision[0], streams, axis=0),
            jnp.take(qc_pass[0], streams, axis=0),
            block_coeffs,
        )
        totals = lax.psum(statistics, "obs")
        send_rows, send_channel = jax.vmap(pack_blocks)(block_sums, channel)
        got_rows, got_channel = (
            lax.all_to_all(send_rows, "obs", split_axis=1, concat_axis=1, tiled=True),
            lax.all_to_all(send_channel, "obs", split_axis=1, concat_axis=1, tiled=True),
        )
        normal = jax.vmap(unpack_blocks)(got_rows, got_channel)
        inflation = (totals[:, 0] + PRIOR_WEIGHT) / (totals[:, 1] + PRIOR_WEIGHT)
        info_post = info_prior + normal[:, :tri_count] / inflation[:, None, None]
        beta_post = beta_prior + jax.vmap(solve_packed)(
            info_post, normal[:, tri_count:] / inflation[:, None, None]
        )
        outgoing = jnp.concatenate([beta_post, memory_factor[None, None, :] * info_post], axis=1)
        incoming = from_behind(outgoing, "section", 1)
        return (beta_post, info_post, incoming)

    def fresh_of(streams):
        return jnp.concatenate(
            [jnp.take(prior_coeffs, streams, axis=0), jnp.take(prior_info, streams, axis=0)], axis=1
        )

    coeff_start = jnp.zeros((1, stream_count, pred_count, local_channels), jnp.float32)
    info_start = jnp.zeros((1, stream_count, tri_count, local_channels), jnp.float32)

    def tick_step(t, loop_state):
        incoming, coeff_out, info_out = loop_state
        entry_index = t - section_place
        usable = (entry_index >= 0) & (entry_index < stream_count)
        slot_index = jnp.clip(entry_index, 0, stream_count - 1)
        streams = lax.dynamic_slice_in_dim(stream_order, slot_index, 1, 0)
        state_now = jnp.where(
            (section_place == 0) | jnp.logical_not(usable), fresh_of(streams), incoming
        )
        beta_post, info_post, incoming = window_work(state_now, streams)

        def store_entry(buffer, result):
            current = lax.dynamic_slice_in_dim(buffer, slot_index, 1, 1)
            updated = jnp.where(usable, result[None], current)
            return lax.dynamic_update_slice_in_dim(buffer, updated, slot_index, 1)

        return (incoming, store_entry(coeff_out, beta_post), store_entry(info_out, info_post))

    initial = (jnp.zeros((1, column_count, local_channels), jnp.float32), coeff_start, info_start)
    final_state = lax.fori_loop(0, stream_count + section_count - 1, tick_step, initial)
    return (final_state[1], final_state[2])


def solution(mesh):
    in_specs = (
        P("section", None, None, "obs"),
        P("section", None, "obs"),
        P("section", None, "obs"),
        P("section", None, "obs"),
        P("section", None, "obs"),
        P(),
        P(None, None, "obs"),
        P(None, None, "obs"),
        P("obs"),
    )
    out_specs = (P("section", None, None, "obs"), P("section", None, None, "obs"))
    return jax.shard_map(local, mesh=mesh, in_specs=in_specs, out_specs=out_specs, check_vma=False)
```

profile of v0, /device:TPU:3, one launch (start us, length us, event | category | flops | bytes accessed | tf_op | source)
XLA Modules:
  0.0 681.3 jit_solution(5905409147109336993)
XLA Ops:
  2.9 677.4 %while.38 = (s32[]{:T(128)}, f32[1,230,256]{2,1,0:T(8,128)S(1)}, f32[1,4,20,256]{3,1,2,0:T(4,128)S(1)}, f32[1,4,210,256]{3,1,2,0:T(4,128)S(1)}, s32[]{:T(128)}, ...) while((s32[]{:T(128)}, f32[1,230,256]{2,1,0:T(8,128)S(1)}, ...), condition=%wide.region_8.10_spmd.clone.clone, body=%wide.region_0.9_spmd.sunk.clone.clone.sunk | while | flops 57759508 | bytes 13853709 | solution.py:199
  7.5 5.6 all-to-all-start.1
  15.5 24.6 %all_gather.15 = f32[1,20,2048]{2,1,0:T(8,128)S(1)} all-gather(f32[1,20,256]{2,1,0:T(8,128)S(1)} %slice.5342), channel_id=1, replica_groups=mesh['section'=4,'obs'=8] {'obs'}, dimensions={2}, use_global_device_ids=true | all-gather | bytes 184320 | tf_op jit(solution)/shard_map/while/body/eval_jaxpr/all_gather | solution.py:144
  46.8 17.5 %psum.19 = f32[1,2]{1,0:T(1,128)S(1)} all-reduce(f32[1,2]{1,0:T(1,128)S(1)} %maximum_bitcast_fusion.6), channel_id=1, replica_groups=mesh['section'=4,'obs'=8] {'obs'}, use_global_device_ids=true, to_apply=%region_7.8 | all-reduce | flops 2 | bytes 16 | tf_op jit(solution)/shard_map/while/body/eval_jaxpr/psum | solution.py:156
  67.1 3.4 all-to-all-start
  71.8 4.4 all-to-all-done
  84.1 5.9 dynamic_update_slice.31
  90.0 8.0 %collective-permute-done = f32[1,230,256]{2,1,0:T(8,128)S(1)} collective-permute-done((f32[1,230,256]{2,1,0:T(8,128)S(1)}, f32[1,230,256]{2,1,0:T(8,128)S(1)}, u32[]{:S(2)}, u32[]{:S(2)}) %collective-permute-start) | collective-permute-done | bytes 235552 | tf_op jit(solution)/shard_map/while/body/eval_jaxpr/ppermute | solution.py:14
  102.6 3.3 all-to-all-start.1
  108.3 25.2 %all_gather.15 = f32[1,20,2048]{2,1,0:T(8,128)S(1)} all-gather(f32[1,20,256]{2,1,0:T(8,128)S(1)} %slice.5342), channel_id=1, replica_groups=mesh['section'=4,'obs'=8] {'obs'}, dimensions={2}, use_global_device_ids=true | all-gather | bytes 184320 | tf_op jit(solution)/shard_map/while/body/eval_jaxpr/all_gather | solution.py:144
  140.2 17.2 %psum.19 = f32[1,2]{1,0:T(1,128)S(1)} all-reduce(f32[1,2]{1,0:T(1,128)S(1)} %maximum_bitcast_fusion.6), channel_id=1, replica_groups=mesh['section'=4,'obs'=8] {'obs'}, use_global_device_ids=true, to_apply=%region_7.8 | all-reduce | flops 2 | bytes 16 | tf_op jit(solution)/shard_map/while/body/eval_jaxpr/psum | solution.py:156
  160.3 3.4 all-to-all-start
  164.9 4.4 all-to-all-done
  177.2 5.9 dynamic_update_slice.31
  183.1 11.9 %collective-permute-done = f32[1,230,256]{2,1,0:T(8,128)S(1)} collective-permute-done((f32[1,230,256]{2,1,0:T(8,128)S(1)}, f32[1,230,256]{2,1,0:T(8,128)S(1)}, u32[]{:S(2)}, u32[]{:S(2)}) %collective-permute-start) | collective-permute-done | bytes 235552 | tf_op jit(solution)/shard_map/while/body/eval_jaxpr/ppermute | solution.py:14
  199.6 3.3 all-to-all-start.1
  205.4 25.2 %all_gather.15 = f32[1,20,2048]{2,1,0:T(8,128)S(1)} all-gather(f32[1,20,256]{2,1,0:T(8,128)S(1)} %slice.5342), channel_id=1, replica_groups=mesh['section'=4,'obs'=8] {'obs'}, dimensions={2}, use_global_device_ids=true | all-gather | bytes 184320 | tf_op jit(solution)/shard_map/while/body/eval_jaxpr/all_gather | solution.py:144
  237.3 17.2 %psum.19 = f32[1,2]{1,0:T(1,128)S(1)} all-reduce(f32[1,2]{1,0:T(1,128)S(1)} %maximum_bitcast_fusion.6), channel_id=1, replica_groups=mesh['section'=4,'obs'=8] {'obs'}, use_global_device_ids=true, to_apply=%region_7.8 | all-reduce | flops 2 | bytes 16 | tf_op jit(solution)/shard_map/while/body/eval_jaxpr/psum | solution.py:156
  257.3 3.4 all-to-all-start
  262.0 4.4 all-to-all-done
  274.3 5.9 dynamic_update_slice.31
  280.2 11.9 %collective-permute-done = f32[1,230,256]{2,1,0:T(8,128)S(1)} collective-permute-done((f32[1,230,256]{2,1,0:T(8,128)S(1)}, f32[1,230,256]{2,1,0:T(8,128)S(1)}, u32[]{:S(2)}, u32[]{:S(2)}) %collective-permute-start) | collective-permute-done | bytes 235552 | tf_op jit(solution)/shard_map/while/body/eval_jaxpr/ppermute | solution.py:14
  296.7 3.3 all-to-all-start.1
  302.4 25.2 %all_gather.15 = f32[1,20,2048]{2,1,0:T(8,128)S(1)} all-gather(f32[1,20,256]{2,1,0:T(8,128)S(1)} %slice.5342), channel_id=1, replica_groups=mesh['section'=4,'obs'=8] {'obs'}, dimensions={2}, use_global_device_ids=true | all-gather | bytes 184320 | tf_op jit(solution)/shard_map/while/body/eval_jaxpr/all_gather | solution.py:144
  334.3 17.2 %psum.19 = f32[1,2]{1,0:T(1,128)S(1)} all-reduce(f32[1,2]{1,0:T(1,128)S(1)} %maximum_bitcast_fusion.6), channel_id=1, replica_groups=mesh['section'=4,'obs'=8] {'obs'}, use_global_device_ids=true, to_apply=%region_7.8 | all-reduce | flops 2 | bytes 16 | tf_op jit(solution)/shard_map/while/body/eval_jaxpr/psum | solution.py:156
  354.4 3.4 all-to-all-start
  359.1 4.4 all-to-all-done
  371.3 5.9 dynamic_update_slice.31
  377.2 11.9 %collective-permute-done = f32[1,230,256]{2,1,0:T(8,128)S(1)} collective-permute-done((f32[1,230,256]{2,1,0:T(8,128)S(1)}, f32[1,230,256]{2,1,0:T(8,128)S(1)}, u32[]{:S(2)}, u32[]{:S(2)}) %collective-permute-start) | collective-permute-done | bytes 235552 | tf_op jit(solution)/shard_map/while/body/eval_jaxpr/ppermute | solution.py:14
  393.7 3.3 all-to-all-start.1
  399.5 25.2 %all_gather.15 = f32[1,20,2048]{2,1,0:T(8,128)S(1)} all-gather(f32[1,20,256]{2,1,0:T(8,128)S(1)} %slice.5342), channel_id=1, replica_groups=mesh['section'=4,'obs'=8] {'obs'}, dimensions={2}, use_global_device_ids=true | all-gather | bytes 184320 | tf_op jit(solution)/shard_map/while/body/eval_jaxpr/all_gather | solution.py:144
  431.4 17.2 %psum.19 = f32[1,2]{1,0:T(1,128)S(1)} all-reduce(f32[1,2]{1,0:T(1,128)S(1)} %maximum_bitcast_fusion.6), channel_id=1, replica_groups=mesh['section'=4,'obs'=8] {'obs'}, use_global_device_ids=true, to_apply=%region_7.8 | all-reduce | flops 2 | bytes 16 | tf_op jit(solution)/shard_map/while/body/eval_jaxpr/psum | solution.py:156
  451.5 3.4 all-to-all-start
  456.1 4.4 all-to-all-done
  468.4 5.9 dynamic_update_slice.31
  474.3 11.9 %collective-permute-done = f32[1,230,256]{2,1,0:T(8,128)S(1)} collective-permute-done((f32[1,230,256]{2,1,0:T(8,128)S(1)}, f32[1,230,256]{2,1,0:T(8,128)S(1)}, u32[]{:S(2)}, u32[]{:S(2)}) %collective-permute-start) | collective-permute-done | bytes 235552 | tf_op jit(solution)/shard_map/while/body/eval_jaxpr/ppermute | solution.py:14
  496.5 25.2 %all_gather.15 = f32[1,20,2048]{2,1,0:T(8,128)S(1)} all-gather(f32[1,20,256]{2,1,0:T(8,128)S(1)} %slice.5342), channel_id=1, replica_groups=mesh['section'=4,'obs'=8] {'obs'}, dimensions={2}, use_global_device_ids=true | all-gather | bytes 184320 | tf_op jit(solution)/shard_map/while/body/eval_jaxpr/all_gather | solution.py:144
  528.5 17.2 %psum.19 = f32[1,2]{1,0:T(1,128)S(1)} all-reduce(f32[1,2]{1,0:T(1,128)S(1)} %maximum_bitcast_fusion.6), channel_id=1, replica_groups=mesh['section'=4,'obs'=8] {'obs'}, use_global_device_ids=true, to_apply=%region_7.8 | all-reduce | flops 2 | bytes 16 | tf_op jit(solution)/shard_map/while/body/eval_jaxpr/psum | solution.py:156
  548.5 3.4 all-to-all-start
  553.2 4.4 all-to-all-done
  565.4 5.9 dynamic_update_slice.31
  571.4 11.9 %collective-permute-done = f32[1,230,256]{2,1,0:T(8,128)S(1)} collective-permute-done((f32[1,230,256]{2,1,0:T(8,128)S(1)}, f32[1,230,256]{2,1,0:T(8,128)S(1)}, u32[]{:S(2)}, u32[]{:S(2)}) %collective-permute-start) | collective-permute-done | bytes 235552 | tf_op jit(solution)/shard_map/while/body/eval_jaxpr/ppermute | solution.py:14
  593.6 25.2 %all_gather.15 = f32[1,20,2048]{2,1,0:T(8,128)S(1)} all-gather(f32[1,20,256]{2,1,0:T(8,128)S(1)} %slice.5342), channel_id=1, replica_groups=mesh['section'=4,'obs'=8] {'obs'}, dimensions={2}, use_global_device_ids=true | all-gather | bytes 184320 | tf_op jit(solution)/shard_map/while/body/eval_jaxpr/all_gather | solution.py:144
  625.5 17.2 %psum.19 = f32[1,2]{1,0:T(1,128)S(1)} all-reduce(f32[1,2]{1,0:T(1,128)S(1)} %maximum_bitcast_fusion.6), channel_id=1, replica_groups=mesh['section'=4,'obs'=8] {'obs'}, use_global_device_ids=true, to_apply=%region_7.8 | all-reduce | flops 2 | bytes 16 | tf_op jit(solution)/shard_map/while/body/eval_jaxpr/psum | solution.py:156
  645.6 3.4 all-to-all-start
  650.2 4.4 all-to-all-done
  662.5 5.9 dynamic_update_slice.31
  668.4 11.9 %collective-permute-done = f32[1,230,256]{2,1,0:T(8,128)S(1)} collective-permute-done((f32[1,230,256]{2,1,0:T(8,128)S(1)}, f32[1,230,256]{2,1,0:T(8,128)S(1)}, u32[]{:S(2)}, u32[]{:S(2)}) %collective-permute-start) | collective-permute-done | bytes 235552 | tf_op jit(solution)/shard_map/while/body/eval_jaxpr/ppermute | solution.py:14
  (632 shorter events, 164.7 us)
Async XLA Ops:
  2.2 0.7 copy-start.4
  2.3 0.7 copy-start.5
  2.3 0.7 copy-start.6
  7.5 59.6 %all-to-all-start.1 = ((f32[1,8,8]{2,0,1:T(1,128)}), f32[1,8,8]{2,0,1:T(1,128)S(1)}, u32[]{:S(2)}, u32[]{:S(2)}) async-start(f32[1,8,8]{2,0,1:T(1,128)} %bitcast.2454), calls=%async_computation.1 | async-start | bytes 8192 | tf_op jit(solution)/shard_map/while/body/eval_jaxpr/all_to_all | solution.py:160
  67.1 9.1 %all-to-all-start = ((f32[1,8,8,230]{3,2,0,1:T(8,128)}), f32[1,8,8,230]{3,2,0,1:T(8,128)S(1)}, u32[]{:S(2)}, u32[]{:S(2)}) async-start(f32[1,8,8,230]{3,2,0,1:T(8,128)} %convolution_bitcast_fusion.4), calls=%async_computation | async-start | bytes 131072 | tf_op jit(solution)/shard_map/while/body/eval_jaxpr/all_to_all | solution.py:159
  76.6 0.6 copy-start
  78.0 0.7 slice-start
  79.9 0.7 copy-start.1
  82.4 15.6 %collective-permute-start = (f32[1,230,256]{2,1,0:T(8,128)S(1)}, f32[1,230,256]{2,1,0:T(8,128)S(1)}, u32[]{:S(2)}, u32[]{:S(2)}) collective-permute-start(f32[1,230,256]{2,1,0:T(8,128)S(1)} %pad_maximum_fusion.2), channel_id=1, source_target_pairs={{0,8},{8,16},{16,24},{1,9},{9,17},{17,25},{2,10},{10,18},{18,26},{... | collective-permute-start | bytes 706568 | tf_op jit(solution)/shard_map/while/body/eval_jaxpr/ppermute | solution.py:14
  102.6 57.7 %all-to-all-start.1 = ((f32[1,8,8]{2,0,1:T(1,128)}), f32[1,8,8]{2,0,1:T(1,128)S(1)}, u32[]{:S(2)}, u32[]{:S(2)}) async-start(f32[1,8,8]{2,0,1:T(1,128)} %bitcast.2454), calls=%async_computation.1 | async-start | bytes 8192 | tf_op jit(solution)/shard_map/while/body/eval_jaxpr/all_to_all | solution.py:160
  160.3 9.1 %all-to-all-start = ((f32[1,8,8,230]{3,2,0,1:T(8,128)}), f32[1,8,8,230]{3,2,0,1:T(8,128)S(1)}, u32[]{:S(2)}, u32[]{:S(2)}) async-start(f32[1,8,8,230]{3,2,0,1:T(8,128)} %convolution_bitcast_fusion.4), calls=%async_computation | async-start | bytes 131072 | tf_op jit(solution)/shard_map/while/body/eval_jaxpr/all_to_all | solution.py:159
  169.7 0.6 copy-start
  171.1 0.7 slice-start
  173.0 0.7 copy-start.1
  175.5 19.5 %collective-permute-start = (f32[1,230,256]{2,1,0:T(8,128)S(1)}, f32[1,230,256]{2,1,0:T(8,128)S(1)}, u32[]{:S(2)}, u32[]{:S(2)}) collective-permute-start(f32[1,230,256]{2,1,0:T(8,128)S(1)} %pad_maximum_fusion.2), channel_id=1, source_target_pairs={{0,8},{8,16},{16,24},{1,9},{9,17},{17,25},{2,10},{10,18},{18,26},{... | collective-permute-start | bytes 706568 | tf_op jit(solution)/shard_map/while/body/eval_jaxpr/ppermute | solution.py:14
  199.6 57.7 %all-to-all-start.1 = ((f32[1,8,8]{2,0,1:T(1,128)}), f32[1,8,8]{2,0,1:T(1,128)S(1)}, u32[]{:S(2)}, u32[]{:S(2)}) async-start(f32[1,8,8]{2,0,1:T(1,128)} %bitcast.2454), calls=%async_computation.1 | async-start | bytes 8192 | tf_op jit(solution)/shard_map/while/body/eval_jaxpr/all_to_all | solution.py:160
  257.3 9.1 %all-to-all-start = ((f32[1,8,8,230]{3,2,0,1:T(8,128)}), f32[1,8,8,230]{3,2,0,1:T(8,128)S(1)}, u32[]{:S(2)}, u32[]{:S(2)}) async-start(f32[1,8,8,230]{3,2,0,1:T(8,128)} %convolution_bitcast_fusion.4), calls=%async_computation | async-start | bytes 131072 | tf_op jit(solution)/shard_map/while/body/eval_jaxpr/all_to_all | solution.py:159
  266.8 0.6 copy-start
  268.2 0.7 slice-start
  270.1 0.7 copy-start.1
  272.6 19.5 %collective-permute-start = (f32[1,230,256]{2,1,0:T(8,128)S(1)}, f32[1,230,256]{2,1,0:T(8,128)S(1)}, u32[]{:S(2)}, u32[]{:S(2)}) collective-permute-start(f32[1,230,256]{2,1,0:T(8,128)S(1)} %pad_maximum_fusion.2), channel_id=1, source_target_pairs={{0,8},{8,16},{16,24},{1,9},{9,17},{17,25},{2,10},{10,18},{18,26},{... | collective-permute-start | bytes 706568 | tf_op jit(solution)/shard_map/while/body/eval_jaxpr/ppermute | solution.py:14
  296.7 57.7 %all-to-all-start.1 = ((f32[1,8,8]{2,0,1:T(1,128)}), f32[1,8,8]{2,0,1:T(1,128)S(1)}, u32[]{:S(2)}, u32[]{:S(2)}) async-start(f32[1,8,8]{2,0,1:T(1,128)} %bitcast.2454), calls=%async_computation.1 | async-start | bytes 8192 | tf_op jit(solution)/shard_map/while/body/eval_jaxpr/all_to_all | solution.py:160
  354.4 9.1 %all-to-all-start = ((f32[1,8,8,230]{3,2,0,1:T(8,128)}), f32[1,8,8,230]{3,2,0,1:T(8,128)S(1)}, u32[]{:S(2)}, u32[]{:S(2)}) async-start(f32[1,8,8,230]{3,2,0,1:T(8,128)} %convolution_bitcast_fusion.4), calls=%async_computation | async-start | bytes 131072 | tf_op jit(solution)/shard_map/while/body/eval_jaxpr/all_to_all | solution.py:159
  363.8 0.6 copy-start
  365.3 0.7 slice-start
  367.2 0.7 copy-start.1
  369.6 19.5 %collective-permute-start = (f32[1,230,256]{2,1,0:T(8,128)S(1)}, f32[1,230,256]{2,1,0:T(8,128)S(1)}, u32[]{:S(2)}, u32[]{:S(2)}) collective-permute-start(f32[1,230,256]{2,1,0:T(8,128)S(1)} %pad_maximum_fusion.2), channel_id=1, source_target_pairs={{0,8},{8,16},{16,24},{1,9},{9,17},{17,25},{2,10},{10,18},{18,26},{... | collective-permute-start | bytes 706568 | tf_op jit(solution)/shard_map/while/body/eval_jaxpr/ppermute | solution.py:14
  393.7 57.7 %all-to-all-start.1 = ((f32[1,8,8]{2,0,1:T(1,128)}), f32[1,8,8]{2,0,1:T(1,128)S(1)}, u32[]{:S(2)}, u32[]{:S(2)}) async-start(f32[1,8,8]{2,0,1:T(1,128)} %bitcast.2454), calls=%async_computation.1 | async-start | bytes 8192 | tf_op jit(solution)/shard_map/while/body/eval_jaxpr/all_to_all | solution.py:160
  451.5 9.1 %all-to-all-start = ((f32[1,8,8,230]{3,2,0,1:T(8,128)}), f32[1,8,8,230]{3,2,0,1:T(8,128)S(1)}, u32[]{:S(2)}, u32[]{:S(2)}) async-start(f32[1,8,8,230]{3,2,0,1:T(8,128)} %convolution_bitcast_fusion.4), calls=%async_computation | async-start | bytes 131072 | tf_op jit(solution)/shard_map/while/body/eval_jaxpr/all_to_all | solution.py:159
  460.9 0.6 copy-start
  462.3 0.7 slice-start
  464.2 0.7 copy-start.1
  466.7 19.5 %collective-permute-start = (f32[1,230,256]{2,1,0:T(8,128)S(1)}, f32[1,230,256]{2,1,0:T(8,128)S(1)}, u32[]{:S(2)}, u32[]{:S(2)}) collective-permute-start(f32[1,230,256]{2,1,0:T(8,128)S(1)} %pad_maximum_fusion.2), channel_id=1, source_target_pairs={{0,8},{8,16},{16,24},{1,9},{9,17},{17,25},{2,10},{10,18},{18,26},{... | collective-permute-start | bytes 706568 | tf_op jit(solution)/shard_map/while/body/eval_jaxpr/ppermute | solution.py:14
  490.8 57.7 %all-to-all-start.1 = ((f32[1,8,8]{2,0,1:T(1,128)}), f32[1,8,8]{2,0,1:T(1,128)S(1)}, u32[]{:S(2)}, u32[]{:S(2)}) async-start(f32[1,8,8]{2,0,1:T(1,128)} %bitcast.2454), calls=%async_computation.1 | async-start | bytes 8192 | tf_op jit(solution)/shard_map/while/body/eval_jaxpr/all_to_all | solution.py:160
  548.5 9.1 %all-to-all-start = ((f32[1,8,8,230]{3,2,0,1:T(8,128)}), f32[1,8,8,230]{3,2,0,1:T(8,128)S(1)}, u32[]{:S(2)}, u32[]{:S(2)}) async-start(f32[1,8,8,230]{3,2,0,1:T(8,128)} %convolution_bitcast_fusion.4), calls=%async_computation | async-start | bytes 131072 | tf_op jit(solution)/shard_map/while/body/eval_jaxpr/all_to_all | solution.py:159
  558.0 0.6 copy-start
  559.4 0.7 slice-start
  561.3 0.7 copy-start.1
  563.8 19.5 %collective-permute-start = (f32[1,230,256]{2,1,0:T(8,128)S(1)}, f32[1,230,256]{2,1,0:T(8,128)S(1)}, u32[]{:S(2)}, u32[]{:S(2)}) collective-permute-start(f32[1,230,256]{2,1,0:T(8,128)S(1)} %pad_maximum_fusion.2), channel_id=1, source_target_pairs={{0,8},{8,16},{16,24},{1,9},{9,17},{17,25},{2,10},{10,18},{18,26},{... | collective-permute-start | bytes 706568 | tf_op jit(solution)/shard_map/while/body/eval_jaxpr/ppermute | solution.py:14
  587.9 57.7 %all-to-all-start.1 = ((f32[1,8,8]{2,0,1:T(1,128)}), f32[1,8,8]{2,0,1:T(1,128)S(1)}, u32[]{:S(2)}, u32[]{:S(2)}) async-start(f32[1,8,8]{2,0,1:T(1,128)} %bitcast.2454), calls=%async_computation.1 | async-start | bytes 8192 | tf_op jit(solution)/shard_map/while/body/eval_jaxpr/all_to_all | solution.py:160
  645.6 9.1 %all-to-all-start = ((f32[1,8,8,230]{3,2,0,1:T(8,128)}), f32[1,8,8,230]{3,2,0,1:T(8,128)S(1)}, u32[]{:S(2)}, u32[]{:S(2)}) async-start(f32[1,8,8,230]{3,2,0,1:T(8,128)} %convolution_bitcast_fusion.4), calls=%async_computation | async-start | bytes 131072 | tf_op jit(solution)/shard_map/while/body/eval_jaxpr/all_to_all | solution.py:159
  655.0 0.6 copy-start
  656.4 0.7 slice-start
  658.3 0.7 copy-start.1
  660.8 19.5 %collective-permute-start = (f32[1,230,256]{2,1,0:T(8,128)S(1)}, f32[1,230,256]{2,1,0:T(8,128)S(1)}, u32[]{:S(2)}, u32[]{:S(2)}) collective-permute-start(f32[1,230,256]{2,1,0:T(8,128)S(1)} %pad_maximum_fusion.2), channel_id=1, source_target_pairs={{0,8},{8,16},{16,24},{1,9},{9,17},{17,25},{2,10},{10,18},{18,26},{... | collective-permute-start | bytes 706568 | tf_op jit(solution)/shard_map/while/body/eval_jaxpr/ppermute | solution.py:14
  680.4 0.9 copy-start.2
  680.4 0.9 copy-start.3
where the time goes:
time: 692 us; the launch traced here: 681 us
  blocking collectives  296 us (43%)
  waiting for transfers between devices  111 us (16%)
  local copies, waits for them, and re-layouts  109 us (16%)
  other arithmetic  68.2 us (10%)
  starting transfers between devices  58 us (8%)
  loops' own time  25.5 us (4%)
  matrix products  12.9 us (2%)
    all_gather x7, blocking collectives, window_work(): all_coeffs = lax.all_gather(beta_prior, 'obs', axis=2, tiled=True)  176 us
    psum x7, blocking collectives, window_work(): totals = lax.psum(statistics, 'obs')  120 us
    ppermute x7, waiting for transfers between devices, from_behind(): return lax.ppermute(array, axis, pairs)  79.7 us
    dynamic_update_slice x28, local copies, waits for them, and re-layouts, store_entry(): return lax.dynamic_update_slice_in_dim(buffer, updated, slot_index, 1)  43.8 us
    all_to_all x7, waiting for transfers between devices, window_work(): lax.all_to_all(send_rows, 'obs', split_axis=1, concat_axis=1, tiled=True)  30.8 us
    another operation x1, loops' own time, local(): lax.fori_loop(0, stream_count + section_count - 1, tick_step, initial)  25.5 us
    all_to_all x7, starting transfers between devices, window_work(): lax.all_to_all(send_channel, 'obs', split_axis=1, concat_axis=1, tiled=True)  25.4 us
    all_to_all x7, starting transfers between devices, window_work(): lax.all_to_all(send_rows, 'obs', split_axis=1, concat_axis=1, tiled=True)  23.5 us
  transfers between devices with their start and end apart: 21, of which 14 were waited for; matrix products, arithmetic and copies ran while one was open for 19% of the time, Pallas kernels for 0%

commit v1 on v0

v1 whole, which is shorter than its diff:
```python
import functools

import jax
import jax.numpy as jnp
import numpy as np
from jax import lax
from jax.experimental import pallas as pl
from jax.experimental.pallas import tpu as pltpu
from jax.sharding import PartitionSpec as P

HUBER_SQ = 9.0
PRIOR_WEIGHT = 64.0
F32 = jnp.float32
BF16 = jnp.bfloat16
NN = (((1,), (0,)), ((), ()))
NT = (((1,), (1,)), ((), ()))
TN = (((0,), (0,)), ((), ()))


def round_up(n, m):
    return -(-n // m) * m


def split3(x):
    hi = x.astype(BF16)
    rest = x - hi.astype(F32)
    mid = rest.astype(BF16)
    low = (rest - mid.astype(F32)).astype(BF16)
    return hi, mid, low


def dot(a, b, dims):
    return lax.dot_general(a, b, dims, preferred_element_type=F32)


def kernel(
    cfg,
    order_ref,
    x_ref,
    dep_ref,
    prec_ref,
    qc_ref,
    bc_ref,
    pc_ref,
    pi_ref,
    mf_ref,
    expand_ref,
    pick_ref,
    prefix_ref,
    co_ref,
    io_ref,
    xs,
    bcs,
    bcr,
    cs,
    cr,
    ts,
    tr,
    beta,
    state,
    work,
    info_out,
    beta_out,
    bc_send,
    bc_recv,
    c_send,
    c_recv,
    t_send,
    t_recv,
    o_send,
    o_recv,
):
    S, O, K, N, NP, T, C, NB, SL, TL = cfg
    sec = lax.axis_index("section")
    ob = lax.axis_index("obs")
    owner = sec < K
    mine = jnp.minimum(sec, K - 1)

    def send(src, dst, send_sem, recv_sem, s, o):
        here = (s == sec) & (o == ob)

        @pl.when(jnp.logical_not(here))
        def _():
            pltpu.make_async_remote_copy(
                src_ref=src,
                dst_ref=dst,
                send_sem=send_sem,
                recv_sem=recv_sem,
                device_id={"section": s, "obs": o},
                device_id_type=pl.DeviceIdType.MESH,
            ).start()

        @pl.when(here)
        def _():
            pltpu.make_async_copy(src, dst, recv_sem).start()

    def sent(src, send_sem, s, o):
        @pl.when(jnp.logical_not((s == sec) & (o == ob)))
        def _():
            pltpu.make_async_copy(src, src, send_sem).wait()

    def got(dst, recv_sem):
        pltpu.make_async_copy(dst, dst, recv_sem).wait()

    for k in range(K):
        bcs[k] = jnp.broadcast_to(bc_ref[order_ref[k]], (SL, 128))

    def send_channels(k, _):
        def one(o, _):
            send(bcs.at[k], bcr.at[sec, ob], bc_send.at[k, o], bc_recv.at[sec, ob], k, o)
            return 0

        return lax.fori_loop(0, O, one, 0)

    lax.fori_loop(0, K, send_channels, 0)

    for k in range(K):
        xs[k, 0:N, :] = x_ref[order_ref[k]].astype(F32)
        xs[k, N:NP, :] = jnp.zeros((NP - N, xs.shape[2]), F32)
    beta[...] = jnp.zeros_like(beta)
    beta[0:N, :] = pc_ref[order_ref[mine]]
    state[...] = pi_ref[order_ref[mine]]

    rows8 = lax.broadcasted_iota(jnp.int32, (O * SL, 128), 0)
    rank_of_row = (rows8 % SL + 1).astype(F32)

    def slots(channel, low):
        inside = (channel >= low) & (channel < low + C)
        rank = dot(jnp.where(inside, 1.0, 0.0).astype(BF16), prefix_ref[...], NN)
        return inside & (rank == rank_of_row)

    @pl.when(owner)
    def _():
        def arrive(w, _):
            def one(o, _):
                got(bcr.at[w, o], bc_recv.at[w, o])
                return 0

            return lax.fori_loop(0, O, one, 0)

        lax.fori_loop(0, S, arrive, 0)

    def row_entry(k, w):
        m = order_ref[k]
        placing = slots(
            jnp.broadcast_to(bc_ref[m], (O * SL, 128)), (rows8 // SL) * C
        )
        placing = jnp.where(placing, 1.0, 0.0).astype(BF16)

        def one(o, _):
            got(cr.at[k, o], c_recv.at[k, o])
            return 0

        lax.fori_loop(0, O, one, 0)
        parts = split3(cr[k].reshape(O * SL, 128))
        coef3 = jnp.concatenate(
            [dot(placing, part, TN)[0:NB, 0:NP] for part in parts], axis=0
        ).astype(BF16)
        sub = lax.broadcasted_iota(jnp.int32, (8, 128), 0)
        tiles = [jnp.zeros((8, 128), F32) for _ in range(NB // 8)]
        blocks = []
        for b in range(NB):
            xb = xs[k, :, b * 128 : (b + 1) * 128]
            xh = xb.astype(BF16)
            blocks.append(xb)
            full = dot(coef3, xh, NN)
            q = b // 8 * 8
            tile = full[q : q + 8] + full[NB + q : NB + q + 8] + full[2 * NB + q : 2 * NB + q + 8]
            tiles[b // 8] = jnp.where(sub == b % 8, tile, tiles[b // 8])
        offset = jnp.concatenate(tiles, axis=0)
        residual = dep_ref[m] - offset
        precision = prec_ref[m]
        passed = qc_ref[m].astype(F32)
        weight = passed * precision / (1.0 + precision * residual * residual / HUBER_SQ)
        total = jnp.sum(jnp.sum(weight * residual * residual, axis=0, keepdims=True), axis=1, keepdims=True)
        count = jnp.sum(jnp.sum(passed, axis=0, keepdims=True), axis=1, keepdims=True)
        pieces = [p.astype(F32) for p in split3(residual)]
        line = lax.broadcasted_iota(jnp.int32, (NP, 128), 0)
        grams = []
        for b in range(NB):
            xb = blocks[b]
            left = (weight[b : b + 1] * xb).astype(BF16)
            right = xb
            for p in range(3):
                right = jnp.where(line == N + p, pieces[p][b : b + 1], right)
            grams.append(dot(left, right.astype(BF16), NT))
        gram = jnp.concatenate(grams, axis=0)
        spread = sum(dot(part, expand_ref[...], NN) for part in split3(gram))
        packed = jnp.sum(spread.reshape(NB, NP, TL) * pick_ref[...][None], axis=1)
        out = sum(dot(placing[:, 0:NB], part, NN) for part in split3(packed))
        lane = lax.broadcasted_iota(jnp.int32, (O * SL, TL), 1)
        out = jnp.where(lane == T + N, total, jnp.where(lane == T + N + 1, count, out))
        ts[k] = out.reshape(O, SL, TL)

        def push(o, _):
            send(ts.at[k, o], tr.at[w, ob], t_send.at[k, o], t_recv.at[w, ob], k, o)
            return 0

        lax.fori_loop(0, O, push, 0)

    def owner_slots(w):
        channel = bcr[w].reshape(O * SL, 128)
        low = ob * C
        hit = slots(channel, low)
        value = jnp.sum(jnp.where(hit, (channel - low + 1).astype(F32), 0.0), axis=1, keepdims=True)
        lane = lax.broadcasted_iota(jnp.int32, (O * SL, C), 1).astype(F32)
        return jnp.where(lane == value - 1.0, 1.0, 0.0).astype(BF16)

    def solve(w):
        hot = owner_slots(w)

        def one(o, _):
            got(tr.at[w, o], t_recv.at[w, o])
            return 0

        lax.fori_loop(0, O, one, 0)
        terms = tr[w].reshape(O * SL, TL)
        row = lax.broadcasted_iota(jnp.int32, (O * SL, TL), 0)
        sums = jnp.sum(jnp.where(row % SL == 0, terms, 0.0), axis=0, keepdims=True)
        inverse = (sums[:, T + N + 1 : T + N + 2] + PRIOR_WEIGHT) / (sums[:, T + N : T + N + 1] + PRIOR_WEIGHT)
        normal = sum(dot(part, hot, TN) for part in split3(terms)) * inverse
        post = state[...] + normal[0:T]
        work[0:T, :] = post
        work[T:TL, :] = normal[T:TL]
        info_out[w] = post
        state[...] = post * mf_ref[...]
        send(info_out.at[w], io_ref.at[sec], o_send.at[w, 0], o_recv.at[sec, 0], w, ob)
        cols = []
        for k in range(N):
            at = k * N - k * (k - 1) // 2 - k
            cols.append(work[at : at + NP, :])
        target = work[T : T + NP, :]
        scales, forward, starts = [], [], [0] * N
        for j in range(N):
            scale = lax.rsqrt(cols[j][j - starts[j] : j - starts[j] + 1])
            scales.append(scale)
            base = j // 8 * 8
            factor = cols[j][base - starts[j] :] * scale
            cols[j] = factor
            starts[j] = base
            step = target[j : j + 1] * scale
            forward.append(step)
            target = target - jnp.concatenate([jnp.zeros((base, C), F32), factor * step], axis=0) if base else target - factor * step
            for k in range(j + 1, N):
                kb = k // 8 * 8
                cols[k] = cols[k][kb - starts[k] :] - factor[kb - base :] * factor[k - base : k - base + 1]
                starts[k] = kb
        index = lax.broadcasted_iota(jnp.int32, (NP, C), 0)
        answer = jnp.zeros((NP, C), F32)
        for i in reversed(range(N)):
            base = i // 8 * 8
            dots = jnp.sum(cols[i] * answer[base:], axis=0, keepdims=True)
            value = (forward[i] - dots) * scales[i]
            answer = jnp.where(index == i, value, answer)
        fresh = beta[0:N, :] + answer[0:N]
        beta[0:N, :] = fresh
        beta_out[w] = fresh
        send(beta_out.at[w], co_ref.at[sec], o_send.at[w, 1], o_recv.at[sec, 1], w, ob)

    def window(w, _):
        @pl.when(owner)
        def _():
            hot = owner_slots(w)
            cs[w] = sum(dot(hot, part, NT) for part in split3(beta[...])).reshape(O, SL, 128)

            def one(o, _):
                send(cs.at[w, o], cr.at[sec, ob], c_send.at[w, o], c_recv.at[sec, ob], w, o)
                return 0

            lax.fori_loop(0, O, one, 0)

        @pl.when(sec == w)
        def _():
            def entry(i, _):
                row_entry((w + 1 + i) % K, w)
                return 0

            lax.fori_loop(0, K, entry, 0)

        @pl.when(owner)
        def _():
            solve(w)

        return 0

    lax.fori_loop(0, S, window, 0)

    for k in range(K):
        got(io_ref.at[k], o_recv.at[k, 0])
        got(co_ref.at[k], o_recv.at[k, 1])

    def drain_rows(k, _):
        def one(o, _):
            sent(bcs.at[k], bc_send.at[k, o], k, o)
            sent(ts.at[k, o], t_send.at[k, o], k, o)
            return 0

        return lax.fori_loop(0, O, one, 0)

    lax.fori_loop(0, K, drain_rows, 0)

    @pl.when(owner)
    def _():
        def drain(w, _):
            def one(o, _):
                sent(cs.at[w, o], c_send.at[w, o], w, o)
                return 0

            lax.fori_loop(0, O, one, 0)
            sent(info_out.at[w], o_send.at[w, 0], w, ob)
            sent(beta_out.at[w], o_send.at[w, 1], w, ob)
            return 0

        lax.fori_loop(0, S, drain, 0)


def local(
    predictors,
    departures,
    obs_precision,
    qc_pass,
    block_channel,
    stream_order,
    prior_coeffs,
    prior_info,
    memory_factor,
):
    S, O = lax.axis_size("section"), lax.axis_size("obs")
    K, N, C = prior_coeffs.shape
    T = prior_info.shape[1]
    NB = block_channel.shape[2]
    R = predictors.shape[3]
    width = R // NB
    assert width == 128 and K <= S and NB <= 128 and NB % 8 == 0
    NP = round_up(N + 3, 8)
    SL = round_up(max(2 * NB // O, 1), 8)
    TL = round_up(T + N + 4, 128)
    pairs = [(i, j) for i in range(N) for j in range(i, N)]
    expand = np.zeros((NP, TL), np.float32)
    pick = np.zeros((NP, TL), np.float32)
    for t, (i, j) in enumerate(pairs):
        expand[j, t] = 1.0
        pick[i, t] = 1.0
    for i in range(N):
        expand[N : N + 3, T + i] = 1.0
        pick[i, T + i] = 1.0
    prefix = (np.arange(128)[:, None] <= np.arange(128)[None, :]).astype(np.float32)
    cfg = (S, O, K, N, NP, T, C, NB, SL, TL)
    channel = jnp.pad(block_channel[0], ((0, 0), (0, 128 - NB)), constant_values=-1)
    vm = pl.BlockSpec(memory_space=pltpu.VMEM)
    dma = pltpu.SemaphoreType.DMA
    coeffs, info = pl.pallas_call(
        functools.partial(kernel, cfg),
        out_shape=(
            jax.ShapeDtypeStruct((K, N, C), F32),
            jax.ShapeDtypeStruct((K, T, C), F32),
        ),
        in_specs=[pl.BlockSpec(memory_space=pltpu.SMEM)] + [vm] * 11,
        out_specs=(vm, vm),
        scratch_shapes=[
            pltpu.VMEM((K, NP, R), F32),
            pltpu.VMEM((K, SL, 128), jnp.int32),
            pltpu.VMEM((S, O, SL, 128), jnp.int32),
            pltpu.VMEM((S, O, SL, 128), F32),
            pltpu.VMEM((K, O, SL, 128), F32),
            pltpu.VMEM((K, O, SL, TL), F32),
            pltpu.VMEM((S, O, SL, TL), F32),
            pltpu.VMEM((128, C), F32),
            pltpu.VMEM((T, C), F32),
            pltpu.VMEM((TL, C), F32),
            pltpu.VMEM((S, T, C), F32),
            pltpu.VMEM((S, N, C), F32),
            dma((K, O)),
            dma((S, O)),
            dma((S, O)),
            dma((K, O)),
            dma((K, O)),
            dma((S, O)),
            dma((S, 2)),
            dma((K, 2)),
        ],
        compiler_params=pltpu.CompilerParams(
            has_side_effects=True, vmem_limit_bytes=60 * 1024 * 1024
        ),
    )(
        stream_order,
        predictors[0],
        departures[0].reshape(K, NB, width),
        obs_precision[0].reshape(K, NB, width),
        qc_pass[0].reshape(K, NB, width),
        channel.reshape(K, 1, 128),
        prior_coeffs,
        prior_info,
        memory_factor[None],
        jnp.asarray(expand, BF16),
        jnp.asarray(pick, F32),
        jnp.asarray(prefix, BF16),
    )
    return coeffs[None], info[None]


def solution(mesh):
    in_specs = (
        P("section", None, None, "obs"),
        P("section", None, "obs"),
        P("section", None, "obs"),
        P("section", None, "obs"),
        P("section", None, "obs"),
        P(),
        P(None, None, "obs"),
        P(None, None, "obs"),
        P("obs"),
    )
    out_specs = (P("section", None, None, "obs"), P("section", None, None, "obs"))
    return jax.shard_map(local, mesh=mesh, in_specs=in_specs, out_specs=out_specs, check_vma=False)
```

time: 692 us -> 92.6 us (0.13); the launches traced: 681 us -> 92.2 us
  blocking collectives: 296 us -> 0 us
  waiting for transfers between devices: 111 us -> 0 us
  local copies, waits for them, and re-layouts: 109 us -> 11.7 us
  Pallas kernels: 0 us -> 79.8 us
  other arithmetic: 68.2 us -> 0 us
  starting transfers between devices: 58 us -> 0 us
  loops' own time: 25.5 us -> 0 us
  matrix products: 12.9 us -> 0 us
    all_gather x7 -> x0, blocking collectives: 176 us -> none  [window_work(): all_coeffs = lax.all_gather(beta_prior, 'obs', axis=2, tiled=True)]
    psum x7 -> x0, blocking collectives: 120 us -> none  [window_work(): totals = lax.psum(statistics, 'obs')]
    pallas_call x0 -> x1, Pallas kernels: none -> 79.8 us  [local(): pl.pallas_call(functools.partial(kernel, cfg), out_shape=(jax.ShapeDtypeS...]
    ppermute x7 -> x0, waiting for transfers between devices: 79.7 us -> none  [from_behind(): return lax.ppermute(array, axis, pairs)]
    all_to_all x14 -> x0, starting transfers between devices: 49 us -> none  [the longest x7 25.4 us: window_work(): lax.all_to_all(send_channel, 'obs', split_axis=1, concat_axis=1, tiled=True)]
    dynamic_update_slice x28 -> x0, local copies, waits for them, and re-layouts: 43.8 us -> none  [store_entry(): return lax.dynamic_update_slice_in_dim(buffer, updated, slot_index, 1)]
    all_to_all x14 -> x0, waiting for transfers between devices: 30.8 us -> none  [the longest x7 30.8 us: window_work(): lax.all_to_all(send_rows, 'obs', split_axis=1, concat_axis=1, tiled=True)]
    gather x42 -> x0, local copies, waits for them, and re-layouts: 25.9 us -> none  [the longest x7 9.46 us: fresh_of(): jnp.take(prior_info, streams, axis=0)]
  transfers between devices with their start and end apart: 21 -> 0, of which waited for: 14 -> 0; matrix products, arithmetic and copies ran while one was open for 19% -> 0% of each run, Pallas kernels for 0% -> 0%
where the time goes in v1:
time: 92.6 us; the launch traced here: 92.2 us
  Pallas kernels  79.8 us (86%)
  local copies, waits for them, and re-layouts  11.7 us (13%)
    pallas_call x1, Pallas kernels, local(): pl.pallas_call(functools.partial(kernel, cfg), out_shape=(jax.ShapeDtypeS...  79.8 us
    unnamed x14, local copies, waits for them, and re-layouts  9.76 us

profile of v1, /device:TPU:3, one launch (start us, length us, event | category | flops | bytes accessed | tf_op | source)
XLA Modules:
  0.0 92.2 jit_solution(5555619555405079810)
XLA Ops:
  0.6 0.0 copy-start.1
  0.6 1.3 %pad.4 = s32[4,128]{1,0:T(4,128)} pad(s32[4,32]{1,0:T(4,128)} %bitcast.29, s32[]{:T(128)} %constant.3.clone.1), padding=0_0x0_96 | pad | bytes 2564 | tf_op jit(solution)/shard_map/jit(_pad)/pad | solution.py:349
  2.0 1.5 %copy.27 = s32[1,4,32,128]{3,2,1,0:T(8,128)} copy(s32[1,4,32,128]{3,1,2,0:T(4,128)} %bitcast.25) | data formatting | bytes 131072
  3.4 0.0 copy-done.1
  3.4 0.0 copy-start.2
  3.4 0.0 copy-start.3
  3.4 0.6 copy.15.pc_ref
  4.1 0.2 copy-done.2
  4.3 0.1 copy-done.3
  4.3 0.0 copy-start
  4.3 0.6 copy_bitcast_fusion.2
  5.0 2.3 %copy.26 = bf16[1,4,20,4096]{3,2,1,0:T(8,128)(2,1)} copy(bf16[1,4,20,4096]{3,1,2,0:T(4,128)(2,1)} %param.12) | data formatting | bytes 1310720 | tf_op args[0]
  7.3 0.0 copy-done
  7.3 1.1 %copy.16.pi_ref = f32[4,210,256]{2,1,0:T(8,128)} copy(f32[4,210,256]{2,0,1:T(4,128)S(1)} %copy-done) | data formatting | bytes 1720320 | tf_op args[7]
  8.4 79.8 %shard_map.131 = (f32[4,20,256]{2,1,0:T(8,128)}, f32[4,210,256]{2,1,0:T(8,128)}) custom-call(s32[4]{0:T(128)} %order_ref.1, bf16[4,20,4096]{2,1,0:T(8,128)(2,1)} %bitcast.21, f32[4,32,128]{2,1,0:T(8,128)} %get-tuple-element.9.dep_ref, f32[4,32,128]{2,1,0:T(8,128)} %get-tuple-element.8.prec_ref, s32[4,32,128]{2,1,0:T(8,128)} %bitcast.23, ...), custom_call_target="tpu_custom_call" | custom-call | tf_op jit(solution)/shard_map/pallas_call | solution.py:352
  88.2 1.6 %copy.17 = f32[1,4,20,256]{3,1,2,0:T(4,128)} copy(f32[1,4,20,256]{3,2,1,0:T(8,128)} %bitcast.24) | data formatting | bytes 163840
  89.8 2.4 %copy.18 = f32[1,4,210,256]{3,1,2,0:T(4,128)} copy(f32[1,4,210,256]{3,2,1,0:T(8,128)} %bitcast.22) | data formatting | bytes 1720320
Async XLA Ops:
  0.6 2.8 %copy-start.1 = (f32[4,20,256]{2,0,1:T(4,128)S(1)}, f32[4,20,256]{2,0,1:T(4,128)}, u32[]{:S(2)}) copy-start(f32[4,20,256]{2,0,1:T(4,128)} %param.18) | copy-start | bytes 245764
  3.4 0.8 copy-start.2
  3.4 0.9 copy-start.3
  4.3 3.0 %copy-start = (f32[4,210,256]{2,0,1:T(4,128)S(1)}, f32[4,210,256]{2,0,1:T(4,128)}, u32[]{:S(2)}) copy-start(f32[4,210,256]{2,0,1:T(4,128)} %param.19) | copy-start | bytes 2580484

commit v2 on v1

--- a/solution.py
+++ b/solution.py
@@ -206,6 +206,9 @@
         lane = lax.broadcasted_iota(jnp.int32, (O * SL, C), 1).astype(F32)
         return jnp.where(lane == value - 1.0, 1.0, 0.0).astype(BF16)
 
+    def send_info(w):
+        send(info_out.at[w], io_ref.at[sec], o_send.at[w, 0], o_recv.at[sec, 0], w, ob)
+
     def solve(w):
         hot = owner_slots(w)
 
@@ -224,7 +227,11 @@
         work[T:TL, :] = normal[T:TL]
         info_out[w] = post
         state[...] = post * mf_ref[...]
-        send(info_out.at[w], io_ref.at[sec], o_send.at[w, 0], o_recv.at[sec, 0], w, ob)
+
+        @pl.when(w == S - 1)
+        def _():
+            send_info(w)
+
         cols = []
         for k in range(N):
             at = k * N - k * (k - 1) // 2 - k
@@ -276,6 +283,10 @@
                 return 0
 
             lax.fori_loop(0, K, entry, 0)
+
+        @pl.when(owner & (w > 0))
+        def _():
+            send_info(w - 1)
 
         @pl.when(owner)
         def _():

time: 92.6 us -> 88.1 us (0.951)
  Pallas kernels: 79.8 us -> 75.3 us
    pallas_call x1, Pallas kernels: 79.8 us -> 75.3 us  [local(): pl.pallas_call(functools.partial(kernel, cfg), out_shape=(jax.ShapeDtypeS...]
where the time goes in v2:
time: 88.1 us; the launch traced here: 87.7 us
  Pallas kernels  75.3 us (85%)
  local copies, waits for them, and re-layouts  11.7 us (13%)
    pallas_call x1, Pallas kernels, local(): pl.pallas_call(functools.partial(kernel, cfg), out_shape=(jax.ShapeDtypeS...  75.3 us
    unnamed x14, local copies, waits for them, and re-layouts  9.76 us

profile of v2, /device:TPU:3, one launch (start us, length us, event | category | flops | bytes accessed | tf_op | source)
XLA Modules:
  0.0 87.7 jit_solution(13117663664983058801)
XLA Ops:
  0.6 0.0 copy-start.1
  0.6 1.3 %pad.4 = s32[4,128]{1,0:T(4,128)} pad(s32[4,32]{1,0:T(4,128)} %bitcast.29, s32[]{:T(128)} %constant.3.clone.1), padding=0_0x0_96 | pad | bytes 2564 | tf_op jit(solution)/shard_map/jit(_pad)/pad | solution.py:360
  2.0 1.5 %copy.27 = s32[1,4,32,128]{3,2,1,0:T(8,128)} copy(s32[1,4,32,128]{3,1,2,0:T(4,128)} %bitcast.25) | data formatting | bytes 131072
  3.4 0.0 copy-done.1
  3.4 0.0 copy-start.2
  3.4 0.0 copy-start.3
  3.4 0.6 copy.15.pc_ref
  4.1 0.2 copy-done.2
  4.3 0.1 copy-done.3
  4.3 0.0 copy-start
  4.3 0.6 copy_bitcast_fusion.2
  5.0 2.3 %copy.26 = bf16[1,4,20,4096]{3,2,1,0:T(8,128)(2,1)} copy(bf16[1,4,20,4096]{3,1,2,0:T(4,128)(2,1)} %param.12) | data formatting | bytes 1310720 | tf_op args[0]
  7.3 0.0 copy-done
  7.3 1.1 %copy.16.pi_ref = f32[4,210,256]{2,1,0:T(8,128)} copy(f32[4,210,256]{2,0,1:T(4,128)S(1)} %copy-done) | data formatting | bytes 1720320 | tf_op args[7]
  8.4 75.3 %shard_map.131 = (f32[4,20,256]{2,1,0:T(8,128)}, f32[4,210,256]{2,1,0:T(8,128)}) custom-call(s32[4]{0:T(128)} %order_ref.1, bf16[4,20,4096]{2,1,0:T(8,128)(2,1)} %bitcast.21, f32[4,32,128]{2,1,0:T(8,128)} %get-tuple-element.9.dep_ref, f32[4,32,128]{2,1,0:T(8,128)} %get-tuple-element.8.prec_ref, s32[4,32,128]{2,1,0:T(8,128)} %bitcast.23, ...), custom_call_target="tpu_custom_call" | custom-call | tf_op jit(solution)/shard_map/pallas_call | solution.py:363
  83.7 1.6 %copy.17 = f32[1,4,20,256]{3,1,2,0:T(4,128)} copy(f32[1,4,20,256]{3,2,1,0:T(8,128)} %bitcast.24) | data formatting | bytes 163840
  85.3 2.4 %copy.18 = f32[1,4,210,256]{3,1,2,0:T(4,128)} copy(f32[1,4,210,256]{3,2,1,0:T(8,128)} %bitcast.22) | data formatting | bytes 1720320
Async XLA Ops:
  0.6 2.8 %copy-start.1 = (f32[4,20,256]{2,0,1:T(4,128)S(1)}, f32[4,20,256]{2,0,1:T(4,128)}, u32[]{:S(2)}) copy-start(f32[4,20,256]{2,0,1:T(4,128)} %param.18) | copy-start | bytes 245764
  3.4 0.8 copy-start.2
  3.4 0.9 %copy-start.3 = (f32[1,4,4096]{2,1,0:T(4,128)S(1)}, f32[1,4,4096]{2,1,0:T(4,128)}, u32[]{:S(2)}) copy-start(f32[1,4,4096]{2,1,0:T(4,128)} %param.13) | copy-start | bytes 196612
  4.3 3.0 %copy-start = (f32[4,210,256]{2,0,1:T(4,128)S(1)}, f32[4,210,256]{2,0,1:T(4,128)}, u32[]{:S(2)}) copy-start(f32[4,210,256]{2,0,1:T(4,128)} %param.19) | copy-start | bytes 2580484

commit v3 on v2

--- a/solution.py
+++ b/solution.py
@@ -47,6 +47,8 @@
     expand_ref,
     pick_ref,
     prefix_ref,
+    co_out,
+    io_out,
     co_ref,
     io_ref,
     xs,
@@ -102,8 +104,44 @@
     def got(dst, recv_sem):
         pltpu.make_async_copy(dst, dst, recv_sem).wait()
 
+    def choose(m, load):
+        value = load(0)
+        for i in range(1, K):
+            value = jnp.where(m == i, load(i), value)
+        return value
+
+    barrier = pltpu.get_barrier_semaphore()
+
+    def greet(s, _):
+        def one(o, _):
+            @pl.when(jnp.logical_not((s == sec) & (o == ob)))
+            def _():
+                pl.semaphore_signal(
+                    barrier,
+                    inc=1,
+                    device_id={"section": s, "obs": o},
+                    device_id_type=pl.DeviceIdType.MESH,
+                )
+
+            return 0
+
+        return lax.fori_loop(0, O, one, 0)
+
+    lax.fori_loop(0, S, greet, 0)
     for k in range(K):
-        bcs[k] = jnp.broadcast_to(bc_ref[order_ref[k]], (SL, 128))
+        line = choose(order_ref[k], lambda i: bc_ref[i : i + 1, :])
+        if NB < 128:
+            line = jnp.concatenate([line, jnp.full((1, 128 - NB), -1, jnp.int32)], axis=1)
+        bcs[k] = jnp.broadcast_to(line, (SL, 128))
+    for b in range(NB):
+        for i in range(N):
+            xs[b, i * K : (i + 1) * K, :] = x_ref[i, :, b * 128 : (b + 1) * 128].astype(F32)
+        xs[b, N * K :, :] = jnp.zeros(((NP - N) * K, 128), F32)
+    beta[...] = jnp.zeros_like(beta)
+    beta[0:N, :] = choose(order_ref[mine], lambda i: pc_ref[:, i, :])
+
+    pl.semaphore_wait(barrier, S * O - 1)
+
 
     def send_channels(k, _):
         def one(o, _):
@@ -113,13 +151,6 @@
         return lax.fori_loop(0, O, one, 0)
 
     lax.fori_loop(0, K, send_channels, 0)
-
-    for k in range(K):
-        xs[k, 0:N, :] = x_ref[order_ref[k]].astype(F32)
-        xs[k, N:NP, :] = jnp.zeros((NP - N, xs.shape[2]), F32)
-    beta[...] = jnp.zeros_like(beta)
-    beta[0:N, :] = pc_ref[order_ref[mine]]
-    state[...] = pi_ref[order_ref[mine]]
 
     rows8 = lax.broadcasted_iota(jnp.int32, (O * SL, 128), 0)
     rank_of_row = (rows8 % SL + 1).astype(F32)
@@ -143,7 +174,7 @@
     def row_entry(k, w):
         m = order_ref[k]
         placing = slots(
-            jnp.broadcast_to(bc_ref[m], (O * SL, 128)), (rows8 // SL) * C
+            jnp.broadcast_to(bcs[k][0:1], (O * SL, 128)), (rows8 // SL) * C
         )
         placing = jnp.where(placing, 1.0, 0.0).astype(BF16)
 
@@ -160,7 +191,7 @@
         tiles = [jnp.zeros((8, 128), F32) for _ in range(NB // 8)]
         blocks = []
         for b in range(NB):
-            xb = xs[k, :, b * 128 : (b + 1) * 128]
+            xb = choose(m, lambda i: xs[b, pl.ds(i, NP, stride=K), :])
             xh = xb.astype(BF16)
             blocks.append(xb)
             full = dot(coef3, xh, NN)
@@ -168,9 +199,9 @@
             tile = full[q : q + 8] + full[NB + q : NB + q + 8] + full[2 * NB + q : 2 * NB + q + 8]
             tiles[b // 8] = jnp.where(sub == b % 8, tile, tiles[b // 8])
         offset = jnp.concatenate(tiles, axis=0)
-        residual = dep_ref[m] - offset
-        precision = prec_ref[m]
-        passed = qc_ref[m].astype(F32)
+        residual = choose(m, lambda i: dep_ref[pl.ds(i, NB, stride=K), :]) - offset
+        precision = choose(m, lambda i: prec_ref[pl.ds(i, NB, stride=K), :])
+        passed = choose(m, lambda i: qc_ref[pl.ds(i, NB, stride=K), :]).astype(F32)
         weight = passed * precision / (1.0 + precision * residual * residual / HUBER_SQ)
         total = jnp.sum(jnp.sum(weight * residual * residual, axis=0, keepdims=True), axis=1, keepdims=True)
         count = jnp.sum(jnp.sum(passed, axis=0, keepdims=True), axis=1, keepdims=True)
@@ -212,6 +243,10 @@
     def solve(w):
         hot = owner_slots(w)
 
+        @pl.when(w == 0)
+        def _():
+            state[...] = choose(order_ref[mine], lambda i: pi_ref[:, i, :])
+
         def one(o, _):
             got(tr.at[w, o], t_recv.at[w, o])
             return 0
@@ -222,6 +257,7 @@
         sums = jnp.sum(jnp.where(row % SL == 0, terms, 0.0), axis=0, keepdims=True)
         inverse = (sums[:, T + N + 1 : T + N + 2] + PRIOR_WEIGHT) / (sums[:, T + N : T + N + 1] + PRIOR_WEIGHT)
         normal = sum(dot(part, hot, TN) for part in split3(terms)) * inverse
+
         post = state[...] + normal[0:T]
         work[0:T, :] = post
         work[T:TL, :] = normal[T:TL]
@@ -298,7 +334,9 @@
 
     for k in range(K):
         got(io_ref.at[k], o_recv.at[k, 0])
+        io_out[:, k, :] = io_ref[k]
         got(co_ref.at[k], o_recv.at[k, 1])
+        co_out[:, k, :] = co_ref[k]
 
     def drain_rows(k, _):
         def one(o, _):
@@ -357,19 +395,24 @@
         pick[i, T + i] = 1.0
     prefix = (np.arange(128)[:, None] <= np.arange(128)[None, :]).astype(np.float32)
     cfg = (S, O, K, N, NP, T, C, NB, SL, TL)
-    channel = jnp.pad(block_channel[0], ((0, 0), (0, 128 - NB)), constant_values=-1)
+
+    def by_block(array):
+        return array[0].reshape(K, NB, width).transpose(1, 0, 2).reshape(NB * K, width)
+
     vm = pl.BlockSpec(memory_space=pltpu.VMEM)
     dma = pltpu.SemaphoreType.DMA
     coeffs, info = pl.pallas_call(
         functools.partial(kernel, cfg),
         out_shape=(
-            jax.ShapeDtypeStruct((K, N, C), F32),
-            jax.ShapeDtypeStruct((K, T, C), F32),
+            jax.ShapeDtypeStruct((N, K, C), F32),
+            jax.ShapeDtypeStruct((T, K, C), F32),
         ),
         in_specs=[pl.BlockSpec(memory_space=pltpu.SMEM)] + [vm] * 11,
         out_specs=(vm, vm),
         scratch_shapes=[
-            pltpu.VMEM((K, NP, R), F32),
+            pltpu.VMEM((K, N, C), F32),
+            pltpu.VMEM((K, T, C), F32),
+            pltpu.VMEM((NB, NP * K, 128), F32),
             pltpu.VMEM((K, SL, 128), jnp.int32),
             pltpu.VMEM((S, O, SL, 128), jnp.int32),
             pltpu.VMEM((S, O, SL, 128), F32),
@@ -391,23 +434,23 @@
             dma((K, 2)),
         ],
         compiler_params=pltpu.CompilerParams(
-            has_side_effects=True, vmem_limit_bytes=60 * 1024 * 1024
+            has_side_effects=True, collective_id=0, vmem_limit_bytes=60 * 1024 * 1024
         ),
     )(
         stream_order,
-        predictors[0],
-        departures[0].reshape(K, NB, width),
-        obs_precision[0].reshape(K, NB, width),
-        qc_pass[0].reshape(K, NB, width),
-        channel.reshape(K, 1, 128),
-        prior_coeffs,
-        prior_info,
+        predictors[0].transpose(1, 0, 2),
+        by_block(departures),
+        by_block(obs_precision),
+        by_block(qc_pass),
+        block_channel[0],
+        prior_coeffs.transpose(1, 0, 2),
+        prior_info.transpose(1, 0, 2),
         memory_factor[None],
         jnp.asarray(expand, BF16),
         jnp.asarray(pick, F32),
         jnp.asarray(prefix, BF16),
     )
-    return coeffs[None], info[None]
+    return coeffs.transpose(1, 0, 2)[None], info.transpose(1, 0, 2)[None]
 
 
 def solution(mesh):

time: 88.1 us -> 76.6 us (0.87)
  local copies, waits for them, and re-layouts: 11.7 us -> 3.74 us
  Pallas kernels: 75.3 us -> 72 us
    unnamed x14 -> x2, local copies, waits for them, and re-layouts: 9.76 us -> 3.74 us
    pallas_call x1, Pallas kernels: 75.3 us -> 72 us  [local(): pl.pallas_call(functools.partial(kernel, cfg), out_shape=(jax.ShapeDtypeS...]
    pad x1 -> x0, local copies, waits for them, and re-layouts: 1.31 us -> none  [local(): jnp.pad(block_channel[0], ((0, 0), (0, 128 - NB)), constant_values=-1)]
where the time goes in v3:
time: 76.6 us; the launch traced here: 76.4 us
  Pallas kernels  72 us (94%)
  local copies, waits for them, and re-layouts  3.74 us (5%)
    pallas_call x1, Pallas kernels, local(): pl.pallas_call(functools.partial(kernel, cfg), out_shape=(jax.ShapeDtypeS...  72 us
    unnamed x2, local copies, waits for them, and re-layouts  3.74 us

profile of v3, /device:TPU:3, one launch (start us, length us, event | category | flops | bytes accessed | tf_op | source)
XLA Modules:
  0.0 76.4 jit_solution(16240600168539002639)
XLA Ops:
  0.6 72.0 %shard_map.131 = (f32[20,4,256]{2,1,0:T(4,128)}, f32[210,4,256]{2,1,0:T(4,128)}) custom-call(s32[4]{0:T(128)} %order_ref.1, bf16[20,4,4096]{2,1,0:T(4,128)(2,1)} %bitcast.30, f32[128,128]{1,0:T(8,128)} %bitcast.33, f32[128,128]{1,0:T(8,128)} %bitcast.34, s32[128,128]{1,0:T(8,128)} %bitcast.35, s32[4,32]{1,0:T(4,128)} %bitcast.36, f32[20,4,256]{2,1,0:T(4,128)} %bitcast.31, ...), custom_call_target="tpu_custom_call" | custom-call | tf_op jit(solution)/shard_map/pallas_call | solution.py:404
  72.6 1.5 %copy.19 = f32[1,4,20,256]{3,1,2,0:T(4,128)} copy(f32[1,4,20,256]{3,1,2,0:T(4,128)} %bitcast.32) | data formatting | bytes 163840
  74.2 2.2 %copy.20 = f32[1,4,210,256]{3,1,2,0:T(4,128)} copy(f32[1,4,210,256]{3,1,2,0:T(4,128)} %bitcast.29) | data formatting | bytes 1720320

commit v4 on v3

--- a/solution.py
+++ b/solution.py
@@ -125,7 +125,7 @@
 
             return 0
 
-        return lax.fori_loop(0, O, one, 0)
+        return lax.fori_loop(0, O, one, 0, unroll=8 if O % 8 == 0 else 1)
 
     lax.fori_loop(0, S, greet, 0)
     for k in range(K):
@@ -148,7 +148,7 @@
             send(bcs.at[k], bcr.at[sec, ob], bc_send.at[k, o], bc_recv.at[sec, ob], k, o)
             return 0
 
-        return lax.fori_loop(0, O, one, 0)
+        return lax.fori_loop(0, O, one, 0, unroll=8 if O % 8 == 0 else 1)
 
     lax.fori_loop(0, K, send_channels, 0)
 
@@ -167,7 +167,7 @@
                 got(bcr.at[w, o], bc_recv.at[w, o])
                 return 0
 
-            return lax.fori_loop(0, O, one, 0)
+            return lax.fori_loop(0, O, one, 0, unroll=8 if O % 8 == 0 else 1)
 
         lax.fori_loop(0, S, arrive, 0)
 
@@ -182,7 +182,7 @@
             got(cr.at[k, o], c_recv.at[k, o])
             return 0
 
-        lax.fori_loop(0, O, one, 0)
+        lax.fori_loop(0, O, one, 0, unroll=8 if O % 8 == 0 else 1)
         parts = split3(cr[k].reshape(O * SL, 128))
         coef3 = jnp.concatenate(
             [dot(placing, part, TN)[0:NB, 0:NP] for part in parts], axis=0
@@ -227,7 +227,7 @@
             send(ts.at[k, o], tr.at[w, ob], t_send.at[k, o], t_recv.at[w, ob], k, o)
             return 0
 
-        lax.fori_loop(0, O, push, 0)
+        lax.fori_loop(0, O, push, 0, unroll=8 if O % 8 == 0 else 1)
 
     def owner_slots(w):
         channel = bcr[w].reshape(O * SL, 128)
@@ -251,7 +251,7 @@
             got(tr.at[w, o], t_recv.at[w, o])
             return 0
 
-        lax.fori_loop(0, O, one, 0)
+        lax.fori_loop(0, O, one, 0, unroll=8 if O % 8 == 0 else 1)
         terms = tr[w].reshape(O * SL, TL)
         row = lax.broadcasted_iota(jnp.int32, (O * SL, TL), 0)
         sums = jnp.sum(jnp.where(row % SL == 0, terms, 0.0), axis=0, keepdims=True)
@@ -310,7 +310,7 @@
                 send(cs.at[w, o], cr.at[sec, ob], c_send.at[w, o], c_recv.at[sec, ob], w, o)
                 return 0
 
-            lax.fori_loop(0, O, one, 0)
+            lax.fori_loop(0, O, one, 0, unroll=8 if O % 8 == 0 else 1)
 
         @pl.when(sec == w)
         def _():
@@ -344,7 +344,7 @@
             sent(ts.at[k, o], t_send.at[k, o], k, o)
             return 0
 
-        return lax.fori_loop(0, O, one, 0)
+        return lax.fori_loop(0, O, one, 0, unroll=8 if O % 8 == 0 else 1)
 
     lax.fori_loop(0, K, drain_rows, 0)
 
@@ -355,7 +355,7 @@
                 sent(cs.at[w, o], c_send.at[w, o], w, o)
                 return 0
 
-            lax.fori_loop(0, O, one, 0)
+            lax.fori_loop(0, O, one, 0, unroll=8 if O % 8 == 0 else 1)
             sent(info_out.at[w], o_send.at[w, 0], w, ob)
             sent(beta_out.at[w], o_send.at[w, 1], w, ob)
             return 0

time: 76.6 us -> 75.6 us (0.987)
  Pallas kernels: 72 us -> 71 us
    pallas_call x1, Pallas kernels: 72 us -> 71 us  [local(): pl.pallas_call(functools.partial(kernel, cfg), out_shape=(jax.ShapeDtypeS...]
where the time goes in v4:
time: 75.6 us; the launch traced here: 75.4 us
  Pallas kernels  71 us (94%)
  local copies, waits for them, and re-layouts  3.74 us (5%)
    pallas_call x1, Pallas kernels, local(): pl.pallas_call(functools.partial(kernel, cfg), out_shape=(jax.ShapeDtypeS...  71 us
    unnamed x2, local copies, waits for them, and re-layouts  3.74 us

profile of v4, /device:TPU:3, one launch (start us, length us, event | category | flops | bytes accessed | tf_op | source)
XLA Modules:
  0.0 75.4 jit_solution(12083808996000699318)
XLA Ops:
  0.6 71.0 %shard_map.131 = (f32[20,4,256]{2,1,0:T(4,128)}, f32[210,4,256]{2,1,0:T(4,128)}) custom-call(s32[4]{0:T(128)} %order_ref.1, bf16[20,4,4096]{2,1,0:T(4,128)(2,1)} %bitcast.30, f32[128,128]{1,0:T(8,128)} %bitcast.33, f32[128,128]{1,0:T(8,128)} %bitcast.34, s32[128,128]{1,0:T(8,128)} %bitcast.35, s32[4,32]{1,0:T(4,128)} %bitcast.36, f32[20,4,256]{2,1,0:T(4,128)} %bitcast.31, ...), custom_call_target="tpu_custom_call" | custom-call | tf_op jit(solution)/shard_map/pallas_call | solution.py:404
  71.7 1.5 %copy.19 = f32[1,4,20,256]{3,1,2,0:T(4,128)} copy(f32[1,4,20,256]{3,1,2,0:T(4,128)} %bitcast.32) | data formatting | bytes 163840
  73.2 2.2 %copy.20 = f32[1,4,210,256]{3,1,2,0:T(4,128)} copy(f32[1,4,210,256]{3,1,2,0:T(4,128)} %bitcast.29) | data formatting | bytes 1720320
